TPU v7x, 256 devices: a whole 4x4x8 slice. The times are simulated.
256 devices in a mesh: row: 8 (over z), col: 32 (over x, y, core).
Axes of the slice: x: 4, y: 4, z: 8, core: 2. Of those that a mesh axis runs over, the one named last changes fastest.
Arguments:
- h_values: float32 [8, 512, 4096], P('row', 'col'), as said below
- h_places: int32 [8, 512], P('row', 'col'), may hold values from 0 to 15, as said below
- h_counts: int32 [8, 32], P('row', 'col'), may hold values from 0 to 16, as said below
- p_values: float32 [8, 512, 4096], P('row', 'col'), as said below
- p_places: int32 [8, 512], P('row', 'col'), may hold values from 0 to 15, as said below
- p_counts: int32 [8, 32], P('row', 'col'), may hold values from 0 to 16, as said below
- s_values: float32 [8, 512, 4096], P('row', 'col'), as said below
- s_places: int32 [8, 512], P('row', 'col'), may hold values from 0 to 15, as said below
- s_counts: int32 [8, 32], P('row', 'col'), may hold values from 0 to 16, as said below
- x_places: int32 [8, 512], P('row', 'col'), may hold values from 0 to 15, as said below
- x_counts: int32 [8, 32], P('row', 'col'), may hold values from 0 to 16, as said below
Outputs:
- gradient: float32 [8, 512, 4096], P('row', 'col')
Inputs may be any that keep to these rules, and one draw needn't show every extreme that they name: `h_places`: in each tile the 16 entries are a permutation of the tile's positions; the first count entries are the present blocks. Every pattern is symmetric, holds every block whose block row and block column lie in the same row panel, and every block (i, j) whose cyclic block distance min(|i - j|, 64 - |i - j|) is 2 or less or exactly 32. `p_places`: as for h_places. `s_places`: as for h_places. `x_places`: as for h_places. `h_counts`: every tile whose block columns lie in its own row panel is full. `p_counts`: as for h_counts. `s_counts`: as for h_counts. `x_counts`: as for h_counts. `h_values`: the assembled H is symmetric. `p_values`: the assembled P is symmetric. `s_values`: the assembled S is symmetric.
All inputs are finite; a program needn't handle non-finite values.
Results may differ from a plain program's by a relative error of at most 0.000088.
Values sent between devices are 32-bit elements; how exact they have to be, the bound alone decides.
A program may use at most 64 MiB of HBM per device.

v0:
```python
import jax
import jax.numpy as jnp
from jax import lax
from jax.sharding import PartitionSpec as P

BS = 64
TC = 2


def from_root(value, axis, source):
    kept = jnp.where(lax.axis_index(axis) == source, value, 0).astype(value.dtype)
    return lax.psum(kept, axis)


def assemble(values, places, counts):
    blocks_in = values[0]
    capacity = blocks_in.shape[0]
    slot_ids = lax.iota(jnp.int32, capacity)
    matches = (places[0][:, None] == slot_ids[None, :]) & (slot_ids[:, None] < counts[0, 0])
    spread = jnp.dot(matches.astype(jnp.float32).T, blocks_in, precision=lax.Precision.HIGHEST)
    row_count = capacity // TC
    return (
        spread.reshape(row_count, TC, BS, BS).transpose(0, 2, 1, 3).reshape(row_count * BS, TC * BS)
    )


def expand_mask(present, row_count, col_count):
    flags = present.reshape(row_count, col_count)
    return jnp.broadcast_to(flags[:, None, :, None], (row_count, BS, col_count, BS)).reshape(
        row_count * BS, col_count * BS
    )


def tile_mask(places, counts):
    capacity = places.shape[1]
    slot_ids = lax.iota(jnp.int32, capacity)
    matches = (places[0][:, None] == slot_ids[None, :]) & (slot_ids[:, None] < counts[0, 0])
    present = jnp.sum(matches.astype(jnp.float32), axis=0)
    return expand_mask(present, capacity // TC, TC)


def tile_to_slots(tile, places, counts):
    row_count = tile.shape[0] // BS
    blocks = (
        tile.reshape(row_count, BS, TC, BS).transpose(0, 2, 1, 3).reshape(row_count * TC, BS * BS)
    )
    picked = jnp.take(blocks, places[0], axis=0)
    slot_ids = lax.iota(jnp.int32, places.shape[1])
    used = (slot_ids < counts[0, 0]).astype(jnp.float32)
    return (picked * used[:, None])[None]


def shards(
    h_values,
    h_places,
    h_counts,
    p_values,
    p_places,
    p_counts,
    s_values,
    s_places,
    s_counts,
    x_places,
    x_counts,
):
    col_index = lax.axis_index("col")
    h_tile = assemble(h_values, h_places, h_counts)
    p_tile = assemble(p_values, p_places, p_counts)
    s_tile = assemble(s_values, s_places, s_counts)
    mask_tile = tile_mask(x_places, x_counts)
    row_width = h_tile.shape[0]
    col_width = h_tile.shape[1]
    p_columns, s_columns = (
        lax.all_gather(p_tile, "row", axis=0, tiled=True),
        lax.all_gather(s_tile, "row", axis=0, tiled=True),
    )
    product = jnp.dot(
        lax.all_gather(h_tile, "col", axis=1, tiled=True),
        p_columns,
        precision=lax.Precision.HIGHEST,
    )
    y_tile = mask_tile * product
    y_panel = lax.all_gather(y_tile, "col", axis=1, tiled=True)
    x_tile = mask_tile * jnp.dot(y_panel, s_columns, precision=lax.Precision.HIGHEST)
    per_panel = row_width // col_width
    source_row = col_index // per_panel
    offset = col_index % per_panel * col_width
    y_part = lax.dynamic_slice_in_dim(y_panel, offset, col_width, 0)
    y_mirror = from_root(y_part, "row", source_row)
    far_part = lax.dot_general(
        lax.all_gather(s_tile, "col", axis=1, tiled=True),
        y_mirror,
        (((1,), (1,)), ((), ())),
        precision=lax.Precision.HIGHEST,
    )
    mirrored = mask_tile * far_part
    return tile_to_slots(x_tile + mirrored, x_places, x_counts)


def solution(mesh):
    in_specs = (
        P("row", "col", None),
        P("row", "col"),
        P("row", "col"),
        P("row", "col", None),
        P("row", "col"),
        P("row", "col"),
        P("row", "col", None),
        P("row", "col"),
        P("row", "col"),
        P("row", "col"),
        P("row", "col"),
    )
    out_specs = P("row", "col", None)
    return jax.shard_map(shards, mesh=mesh, in_specs=in_specs, out_specs=out_specs, check_vma=False)
```

profile of v0, /device:TPU:61, one launch (start us, length us, event | category | flops | bytes accessed | tf_op | source)
XLA Modules:
  0.0 400.5 jit_solution(8840308818379448259)
XLA Ops:
  6.5 0.0 all-gather.8.cloned.1.call-start
  7.3 1.1 dot_general.34
  8.4 0.0 copy-start.2
  8.4 1.3 convolution_bitcast_fusion.1
  9.8 0.3 copy.26
  10.0 0.9 reshape.190
  10.9 0.0 all-gather.8.cloned.1.call-update
  10.9 0.0 all-gather.6.cloned.1.call-start
  11.6 0.0 copy-done
  11.6 0.2 dot_general.31
  11.9 0.0 copy-done.2
  11.9 0.7 convolution_bitcast_fusion.2
  12.6 0.3 copy.24
  12.8 0.9 reshape.189
  13.7 0.0 all-gather.6.cloned.1.call-update
  13.7 0.0 all-gather.10.cloned.1.call-start
  14.4 0.1 convert_reduce_fusion
  14.5 0.1 broadcast_in_dim.19
  14.6 0.2 broadcast_in_dim.20
  14.8 0.3 reshape.188
  15.1 0.0 copy-start.1
  15.2 0.0 copy-start.3
  15.2 34.7 %all-gather.8.cloned.1.call-done = f32[4096,128]{0,1:T(8,128)} async-done(((f32[512,128]{0,1:T(8,128)}), f32[4096,128]{0,1:T(8,128)}) %all-gather.8.cloned.1.call-update) | async-done | bytes 2097168 | tf_op jit(solution)/shard_map/all_gather | solution.py:74
  49.9 62.3 %all-gather.6.cloned.1.call-done = f32[512,4096]{0,1:T(8,128)} async-done(((f32[512,128]{0,1:T(8,128)}), f32[512,4096]{0,1:T(8,128)}) %all-gather.6.cloned.1.call-update) | async-done | bytes 8388624 | tf_op jit(solution)/shard_map/all_gather | solution.py:78
  112.1 16.5 %convolution_multiply_fusion = f32[512,128]{1,0:T(8,128)} fusion(f32[512,128]{1,0:T(8,128)S(1)} %reshape.188, f32[512,4096]{0,1:T(8,128)} %all-gather.6.cloned.1.call-done, f32[4096,128]{0,1:T(8,128)} %all-gather.8.cloned.1.call-done), kind=kOutput, calls=%fused_computation.7 | convolution fusion | flops 3221291008 | bytes 11010048 | tf_op jit(solution)/shard_map/dot_general | solution.py:77
  128.7 0.0 all-gather.10.cloned.1.call-update
  128.7 0.0 all-gather.12.cloned.1.call-start
  129.4 0.0 copy-done.1
  129.4 0.2 dot_general.38
  129.7 0.7 convolution_bitcast_fusion
  130.4 0.3 copy.28
  130.6 0.9 reshape.191
  131.5 0.0 all-gather.12.cloned.1.call-update
  131.5 0.0 all-gather.14.cloned.1.call-start
  131.6 0.5 all-gather.14.cloned.1.call-update
  132.1 0.2 all-reduce.2.cloned.1.call-start
  132.4 60.6 %all-gather.10.cloned.1.call-done = f32[512,4096]{1,0:T(8,128)} async-done(((f32[512,128]{1,0:T(8,128)}), f32[512,4096]{1,0:T(8,128)}) %all-gather.10.cloned.1.call-update) | async-done | bytes 8388624 | tf_op jit(solution)/shard_map/all_gather | solution.py:83
  193.0 3.2 dynamic-slice_select_fusion
  196.1 0.0 all-reduce.2.cloned.1.call-update
  196.2 36.2 %all-gather.12.cloned.1.call-done = f32[4096,128]{0,1:T(8,128)} async-done(((f32[512,128]{0,1:T(8,128)}), f32[4096,128]{0,1:T(8,128)}) %all-gather.12.cloned.1.call-update) | async-done | bytes 2097168 | tf_op jit(solution)/shard_map/all_gather | solution.py:75
  232.4 9.3 %fusion.29 = f32[512,128]{1,0:T(8,128)S(1)} fusion(f32[512,4096]{1,0:T(8,128)} %all-gather.10.cloned.1.call-done, f32[4096,128]{0,1:T(8,128)} %all-gather.12.cloned.1.call-done), kind=kOutput, calls=%fused_computation.48 | convolution fusion | flops 3221225472 | bytes 10747904 | tf_op jit(solution)/shard_map/dot_general | solution.py:84
  241.8 52.8 %all-gather.14.cloned.1.call-done = f32[512,4096]{0,1:T(8,128)} async-done(((f32[512,128]{0,1:T(8,128)}), f32[512,4096]{0,1:T(8,128)}) %all-gather.14.cloned.1.call-update) | async-done | bytes 8388624 | tf_op jit(solution)/shard_map/all_gather | solution.py:91
  294.5 81.2 %all-reduce.2.cloned.1.call-done = f32[128,4096]{1,0:T(8,128)} async-done(((f32[128,4096]{1,0:T(8,128)}), f32[128,4096]{1,0:T(8,128)}) %all-reduce.2.cloned.1.call-update) | async-done | bytes 2097168 | tf_op jit(solution)/shard_map/psum | solution.py:12
  375.7 16.0 %fusion = f32[512,128]{1,0:T(8,128)S(1)} fusion(f32[512,128]{1,0:T(8,128)S(1)} %reshape.188, f32[512,128]{1,0:T(8,128)S(1)} %fusion.29, f32[512,4096]{0,1:T(8,128)} %all-gather.14.cloned.1.call-done, f32[128,4096]{1,0:T(8,128)} %all-reduce.2.cloned.1.call-done), kind=kOutput, calls=%fused_computation.6 | convolution fusion | flops 3221356544 | bytes 11272192 | tf_op jit(solution)/shard_map/dot_general | solution.py:90
  391.7 0.3 reshape.192
  392.1 0.2 reshape.193
  392.3 0.6 gather_fusion
  392.9 0.8 fusion.7
  (13 shorter events, 0.1 us)
Async XLA Ops:
  6.5 5.1 %copy-start = (f32[1,16,4096]{2,1,0:T(8,128)S(1)}, f32[1,16,4096]{2,1,0:T(8,128)}, u32[]{:S(2)}) copy-start(f32[1,16,4096]{2,1,0:T(8,128)} %param.11) | copy-start | bytes 786436
  6.5 43.3 %all-gather.8.cloned.1.call-start = ((), (), s32[]{:S(2)}) async-start(), calls=%async_computation.1 | async-start | bytes 2359296 | tf_op jit(solution)/shard_map/all_gather | solution.py:74
  8.4 3.5 copy-start.2
  10.9 3.5 copy-start.4
  10.9 101.2 %all-gather.6.cloned.1.call-start = ((), (), s32[]{:S(2)}) async-start(), calls=%async_computation | async-start | bytes 8650752 | tf_op jit(solution)/shard_map/all_gather | solution.py:78
  13.7 179.2 %all-gather.10.cloned.1.call-start = ((), (), s32[]{:S(2)}) async-start(), calls=%async_computation.2 | async-start | bytes 8650752 | tf_op jit(solution)/shard_map/all_gather | solution.py:83
  15.1 114.3 %copy-start.1 = (f32[1,16,4096]{2,1,0:T(8,128)S(1)}, f32[1,16,4096]{2,1,0:T(8,128)}, u32[]{:S(2)}) copy-start(f32[1,16,4096]{2,1,0:T(8,128)} %param.17) | copy-start | bytes 786436
  15.2 114.5 %copy-start.3 = (s32[1,16]{1,0:T(1,128)S(1)}, s32[1,16]{1,0:T(1,128)}, u32[]{:S(2)}) copy-start(s32[1,16]{1,0:T(1,128)} %param.18) | copy-start | bytes 196
  128.7 103.7 %all-gather.12.cloned.1.call-start = ((), (), s32[]{:S(2)}) async-start(), calls=%async_computation.3 | async-start | bytes 2359296 | tf_op jit(solution)/shard_map/all_gather | solution.py:75
  131.5 163.0 %all-gather.14.cloned.1.call-start = ((), (), s32[]{:S(2)}) async-start(), calls=%async_computation.4 | async-start | bytes 8650752 | tf_op jit(solution)/shard_map/all_gather | solution.py:91
  132.1 243.6 %all-reduce.2.cloned.1.call-start = ((), (), s32[]{:S(2)}) async-start(), calls=%async_computation.5 | async-start | bytes 4194304 | tf_op jit(solution)/shard_map/psum | solution.py:12
Sparse Core Ops, SparseCore 0:
  11.1 38.7 all-gather.7
  52.4 59.6 all-gather.5
  128.8 64.0 all-gather.9
  194.6 37.7 all-gather.11
  234.8 59.6 all-gather.13
  296.7 78.9 all-reduce.1
where the time goes:
time: 405 us; the launch traced here: 401 us
  waiting for transfers between devices  328 us (81%)
  matrix products  44.6 us (11%)
  between operations  16.4 us (4%)
  local copies, waits for them, and re-layouts  6.76 us (2%)
  other arithmetic  4.09 us (1%)
    psum x1, waiting for transfers between devices, from_root(): return lax.psum(kept, axis)  81.2 us
    all_gather x1, waiting for transfers between devices, shards(): lax.all_gather(h_tile, 'col', axis=1, tiled=True)  62.3 us
    all_gather x1, waiting for transfers between devices, shards(): y_panel = lax.all_gather(y_tile, 'col', axis=1, tiled=True)  60.6 us
    all_gather x1, waiting for transfers between devices, shards(): lax.all_gather(s_tile, 'col', axis=1, tiled=True)  52.8 us
    all_gather x1, waiting for transfers between devices, shards(): lax.all_gather(s_tile, 'row', axis=0, tiled=True)  36.2 us
    all_gather x1, waiting for transfers between devices, shards(): lax.all_gather(p_tile, 'row', axis=0, tiled=True)  34.7 us
    dot_general x1, matrix products, shards(): jnp.dot(lax.all_gather(h_tile, 'col', axis=1, tiled=True), p_columns, pre...  16.5 us
    dot_general x1, matrix products, shards(): lax.dot_general(lax.all_gather(s_tile, 'col', axis=1, tiled=True), y_mirr...  16 us
  transfers between devices with their start and end apart: 6, of which 6 were waited for; matrix products, arithmetic and copies ran while one was open for 4% of the time, Pallas kernels for 0%

commit v1 on v0

v1 whole, which is shorter than its diff:
```python
import jax
import jax.numpy as jnp
from jax import lax
from jax.experimental import pallas as pl
from jax.experimental.pallas import tpu as pltpu
from jax.sharding import PartitionSpec as P

MESH = pl.DeviceIdType.MESH
F32 = jnp.float32
BF16 = jnp.bfloat16
BS = 64
CAP = 16
TILE = 512
WIDTH = 128
HALF = 256
QUARTER = 128
NCOPY = 160


def split(value):
    high = value.astype(BF16)
    return high, (value - high.astype(F32)).astype(BF16)


def kernel(
    index_ref, h_ref, p_ref, s_ref, out_ref,
    hv, pv, sv, hb, yb, pt, st, pb, sb, rhs, acc, part, xt, xs, tr, zt, bl,
    send_sem, recv_sem, local_sem,
):
    z = lax.axis_index("row")
    col = lax.axis_index("col")
    q = lax.rem(col, 2)
    y = lax.rem(col // 2, 4)
    x = col // 8
    lane = lax.broadcasted_iota(jnp.int32, (32, WIDTH), 1)
    low = lane < BS

    def device(dz, dx, dy):
        return (
            lax.rem(z + dz, 8),
            lax.rem(x + dx, 4) * 8 + lax.rem(y + dy, 4) * 2 + q,
        )

    partner = (z, col + 1 - 2 * q)
    mirror_row = col // 4

    def mirror(g):
        return (mirror_row, 4 * z + g)

    diagonal = mirror_row == z
    own_place = lax.rem(col, 4)

    barrier = pltpu.get_barrier_semaphore()
    for target in (
        device(0, 0, 1), device(0, 0, 3), device(0, 1, 0), device(0, 3, 0),
        device(1, 0, 0), device(7, 0, 0), partner,
    ):
        pl.semaphore_signal(barrier, inc=1, device_id=target, device_id_type=MESH)
    for g in range(4):
        @pl.when(jnp.logical_or(mirror_row != z, own_place != g))
        def _(g=g):
            pl.semaphore_signal(barrier, inc=1, device_id=mirror(g), device_id_type=MESH)

    used = {}

    def copy(name, src, dst, target):
        if name not in used:
            used[name] = len(used)
        n = used[name]
        return pltpu.make_async_remote_copy(
            src_ref=src, dst_ref=dst, send_sem=send_sem.at[n], recv_sem=recv_sem.at[n],
            device_id=target, device_id_type=MESH,
        )

    started, gifts = [], []

    def send(name, src, dst, target, kept=None):
        made = copy(name, src, dst, target)
        made.start()
        (started if kept is None else kept).append(made)

    def arrived(name, dst):
        copy(name, dst, dst, partner).wait_recv()

    def place_rows(values, base, dst, index):
        @pl.loop(0, 8)
        def _(i):
            a = values[index_ref[base + 2 * i]]
            b = values[index_ref[base + 2 * i + 1]]
            top = jnp.where(low, a, pltpu.roll(b, BS, 1))
            bottom = jnp.where(low, pltpu.roll(a, BS, 1), b)
            start = pl.multiple_of(i * BS, BS)
            dst[index, pl.ds(start, 32), :] = top
            dst[index, pl.ds(start + 32, 32), :] = bottom

    def place_natural(values, base, dst):
        for i in range(8):
            a = values[index_ref[base + 2 * i]]
            b = values[index_ref[base + 2 * i + 1]]
            even = jnp.where(low, a, pltpu.roll(b, BS, 1))
            odd = jnp.where(low, pltpu.roll(a, BS, 1), b)
            g = i // 2
            view = dst.at[g % 2, g // 2]
            view[pl.ds((i % 2) * BS, 32, 2), :] = even
            view[pl.ds((i % 2) * BS + 1, 32, 2), :] = odd

    for source, values in ((h_ref, hv), (p_ref, pv), (s_ref, sv)):
        values[pl.ds(0, CAP)] = source[...]
        values[CAP] = jnp.zeros((32, WIDTH), F32)
    here = x * 4 + y
    place_rows(hv, 0, hb, here)
    place_natural(pv, CAP, pt)
    place_natural(sv, 2 * CAP, st)

    pl.semaphore_wait(barrier, jnp.where(diagonal, 10, 11))

    def tile_at(first, a, b):
        dy, dx = (a, b) if first == 1 else (b, a)
        return lax.rem(x + dx, 4) * 4 + lax.rem(y + dy, 4)

    def step(first, stage, by):
        along_y = (first == 1) == (stage == 1)
        return device(0, 0, by) if along_y else device(0, by, 0)

    def whole(buf, half, a, b):
        return buf.at[tile_at(1 - half, a, b), pl.ds(half * HALF, HALF)]

    def quarter(buf, half, a, b, k):
        return buf.at[tile_at(1 - half, a, b), pl.ds(half * HALF + k * QUARTER, QUARTER)]

    def first_out(tag, buf, half):
        src = whole(buf, half, 0, 0)
        send((tag, half, "s1", 1), src, src, step(1 - half, 1, 1))
        send((tag, half, "s1", 3), src, src, step(1 - half, 1, 3))

    def second_out(tag, buf, half, a):
        src = whole(buf, half, a, 0)
        send((tag, half, "s2", a, 1), src, src, step(1 - half, 2, 1))
        send((tag, half, "s2", a, 3), src, src, step(1 - half, 2, 3))

    def first_in(tag, buf, half):
        for by, a, k in ((1, 3, 0), (3, 1, 1)):
            arrived((tag, half, "s1", by), whole(buf, half, a, 0))
            src = quarter(buf, half, a, 0, k)
            send((tag, half, "f1", by), src, src, step(1 - half, 1, by))
            second_out(tag, buf, half, a)

    def first_far(tag, buf, half):
        for by, k in ((1, 0), (3, 1)):
            arrived((tag, half, "f1", by), quarter(buf, half, 2, 0, k))
        second_out(tag, buf, half, 2)

    def second_in(tag, buf, half, a):
        for by, b, k in ((1, 3, 0), (3, 1, 1)):
            arrived((tag, half, "s2", a, by), whole(buf, half, a, b))
            src = quarter(buf, half, a, b, k)
            send((tag, half, "f2", a, by), src, src, step(1 - half, 2, by))

    def second_far(tag, buf, half, a):
        for by, k in ((1, 0), (3, 1)):
            arrived((tag, half, "f2", a, by), quarter(buf, half, a, 2, k))

    def ring_start(tag, own, buf):
        keep = pltpu.make_async_copy(own.at[q], buf.at[z, q], local_sem.at[0 if tag == "p" else 1])
        keep.start()
        send((tag, "mate"), own.at[1 - q], buf.at[z, q], partner)
        for by in (1, 7):
            send((tag, "own", by, 1), own.at[q], buf.at[z, q], device(by, 0, 0))
        return keep

    def ring_mate(tag, buf):
        arrived((tag, "mate"), buf.at[z, 1 - q])
        src = buf.at[z, 1 - q]
        for by in (1, 7):
            send((tag, "other", by, 1), src, src, device(by, 0, 0))

    def ring_in(tag, buf, d):
        for kind, core in (("own", q), ("other", 1 - q)):
            for by in (1, 7):
                away = lax.rem(z + (8 - by) * d, 8)
                if d < 4:
                    arrived((tag, kind, by, d), buf.at[away, core])
                if d < 3:
                    src = buf.at[away, core]
                    send((tag, kind, by, d + 1), src, src, device(by, 0, 0))
                elif d == 3:
                    src = buf.at[away, core, 0 if by == 1 else 1]
                    send((tag, kind, by, 4), src, src, device(by, 0, 0))
                else:
                    arrived((tag, kind, by, 4), buf.at[away, core, 0 if by == 1 else 1])

    def weights(buf, away):
        for g in range(2):
            wide = jnp.concatenate([buf[away, 0, g], buf[away, 1, g]], axis=1)
            high, rest = split(wide)
            t = 2 * away + g
            rhs[t, pl.ds(0, 128), :] = high
            rhs[t, pl.ds(128, 128), :] = high
            rhs[t, pl.ds(256, 128), :] = rest

    def weights_at(buf, d):
        @pl.loop(0, 2 if d < 4 else 1)
        def _(k):
            weights(buf, lax.rem(z + jnp.where(k == 0, d, 8 - d), 8))

    def product(buf, half):
        rows = pl.ds(half * HALF, HALF)
        acc[0, rows, :] = jnp.zeros((HALF, WIDTH), F32)
        acc[1, rows, :] = jnp.zeros((HALF, WIDTH), F32)

        @pl.loop(0, 16)
        def _(t):
            high, rest = split(buf[t, rows, :])
            left = jnp.concatenate([high, rest, high], axis=1)
            term = jnp.dot(left, rhs[t], preferred_element_type=F32)
            acc[0, rows, :] += term[:, :WIDTH]
            acc[1, rows, :] += term[:, WIDTH:]

    def give(tag, half):
        rows = pl.ds(half * HALF, HALF)
        send((tag, half), acc.at[1 - q, rows], part.at[0 if tag == "dy" else 1, rows], partner,
             gifts if tag == "dy" else None)

    first_out("h", hb, 0)
    first_out("h", hb, 1)
    keep_p = ring_start("p", pt, pb)
    second_out("h", hb, 0, 0)
    second_out("h", hb, 1, 0)
    ring_mate("p", pb)
    keep_s = ring_start("s", st, sb)
    first_in("h", hb, 0)
    first_in("h", hb, 1)
    keep_p.wait()

    @pl.loop(0, 1)
    def _(k):
        weights(pb, z)

    ring_in("p", pb, 1)
    weights_at(pb, 1)
    first_far("h", hb, 0)
    first_far("h", hb, 1)
    second_in("h", hb, 0, 0)
    second_in("h", hb, 1, 0)
    ring_in("p", pb, 2)
    weights_at(pb, 2)
    for a in (3, 1):
        second_in("h", hb, 0, a)
        second_in("h", hb, 1, a)
    ring_in("p", pb, 3)
    weights_at(pb, 3)
    second_in("h", hb, 0, 2)
    second_in("h", hb, 1, 2)
    ring_mate("s", sb)
    ring_in("s", sb, 1)
    for a in (0, 3, 1, 2):
        second_far("h", hb, 0, a)
        second_far("h", hb, 1, a)
    ring_in("p", pb, 4)
    weights_at(pb, 4)
    product(hb, 0)
    give("dy", 0)
    product(hb, 1)
    give("dy", 1)

    for half in range(2):
        rows = pl.ds(half * HALF, HALF)
        arrived(("dy", half), part.at[0, rows])
        for i in range(4 * half, 4 * half + 4):
            wide = lax.broadcasted_iota(jnp.int32, (BS, WIDTH), 1)
            kept = jnp.where(wide < BS, index_ref[4 * CAP + 2 * i], index_ref[4 * CAP + 2 * i + 1]) > 0
            strip = pl.ds(i * BS, BS)
            yb[here, strip, :] = jnp.where(kept, acc[q, strip, :] + part[0, strip, :], 0.0)
        first_out("y", yb, half)
        second_out("y", yb, half, 0)

    keep_s.wait()

    @pl.loop(0, 1)
    def _(k):
        weights(sb, z)

    weights_at(sb, 1)
    ring_in("s", sb, 2)
    weights_at(sb, 2)
    first_in("y", yb, 0)
    first_in("y", yb, 1)
    first_far("y", yb, 0)
    first_far("y", yb, 1)
    second_in("y", yb, 0, 0)
    second_in("y", yb, 1, 0)
    ring_in("s", sb, 3)
    weights_at(sb, 3)
    for a in (3, 1):
        second_in("y", yb, 0, a)
        second_in("y", yb, 1, a)
    second_in("y", yb, 0, 2)
    second_in("y", yb, 1, 2)
    ring_in("s", sb, 4)
    weights_at(sb, 4)
    for a in (0, 3, 1, 2):
        second_far("y", yb, 0, a)
        second_far("y", yb, 1, a)
    for made in gifts:
        made.wait_send()
    product(yb, 0)
    give("dx", 0)
    product(yb, 1)
    give("dx", 1)

    def chunk(g):
        return pltpu.make_async_remote_copy(
            src_ref=xs.at[g], dst_ref=tr.at[own_place], send_sem=send_sem.at[NCOPY + g],
            recv_sem=recv_sem.at[NCOPY + own_place], device_id=mirror(g), device_id_type=MESH,
        )

    def leaves(g):
        return jnp.logical_or(mirror_row != z, own_place != g)

    for half in range(2):
        arrived(("dx", half), part.at[1, pl.ds(half * HALF, HALF)])
        for g in (2 * half, 2 * half + 1):
            for k in range(2):
                base = g * QUARTER + k * BS
                for odd in range(2):
                    strip = pl.ds(base + 32 * odd, 32)
                    value = acc[q, strip, :] + part[1, strip, :]
                    xt[strip, :] = value
                    xs[g, pl.ds(k * BS + odd, 32, 2), :] = value

            @pl.when(leaves(g))
            def _(g=g):
                chunk(g).start()

            @pl.when(jnp.logical_not(leaves(g)))
            def _(g=g):
                stay = pltpu.make_async_copy(xs.at[g], tr.at[g], local_sem.at[2])
                stay.start()
                stay.wait()

    bl[CAP] = jnp.zeros((32, WIDTH), F32)
    for g in range(4):
        @pl.when(leaves(g))
        def _(g=g):
            pltpu.make_async_remote_copy(
                src_ref=xs.at[g], dst_ref=tr.at[g], send_sem=send_sem.at[NCOPY + g],
                recv_sem=recv_sem.at[NCOPY + g], device_id=mirror(g), device_id_type=MESH,
            ).wait_recv()

        zt[...] = tr[g].T
        for k in range(2):
            i = 2 * g + k
            top = xt[pl.ds(i * BS, 32), :] + zt[pl.ds(k * BS, 32, 2), :]
            bottom = xt[pl.ds(i * BS + 32, 32), :] + zt[pl.ds(k * BS + 1, 32, 2), :]
            bl[2 * i] = jnp.where(low, top, pltpu.roll(bottom, BS, 1))
            bl[2 * i + 1] = jnp.where(low, pltpu.roll(top, BS, 1), bottom)

    @pl.loop(0, CAP)
    def _(slot):
        out_ref[slot] = bl[index_ref[3 * CAP + slot]]

    for g in range(4):
        @pl.when(leaves(g))
        def _(g=g):
            chunk(g).wait_send()

    for made in started:
        made.wait_send()


def shards(
    h_values, h_places, h_counts, p_values, p_places, p_counts,
    s_values, s_places, s_counts, x_places, x_counts,
):
    slots = lax.iota(jnp.int32, CAP)

    def slot_of(places, counts):
        match = (places[0][:, None] == slots[None, :]) & (slots[:, None] < counts[0, 0])
        return jnp.min(jnp.where(match, slots[:, None], CAP), axis=0)

    index = jnp.concatenate([
        slot_of(h_places, h_counts), slot_of(p_places, p_counts), slot_of(s_places, s_counts),
        jnp.where(slots < x_counts[0, 0], x_places[0], CAP),
        (slot_of(x_places, x_counts) < CAP).astype(jnp.int32),
    ])

    def blocks(values):
        return values.reshape(CAP, 32, WIDTH)

    vmem = pl.BlockSpec(memory_space=pltpu.VMEM)
    smem = pl.BlockSpec(memory_space=pltpu.SMEM)
    out = pl.pallas_call(
        kernel,
        out_shape=jax.ShapeDtypeStruct((CAP, 32, WIDTH), F32),
        in_specs=[smem, vmem, vmem, vmem],
        out_specs=vmem,
        scratch_shapes=[
            pltpu.VMEM((CAP + 1, 32, WIDTH), F32),
            pltpu.VMEM((CAP + 1, 32, WIDTH), F32),
            pltpu.VMEM((CAP + 1, 32, WIDTH), F32),
            pltpu.VMEM((16, TILE, WIDTH), F32),
            pltpu.VMEM((16, TILE, WIDTH), F32),
            pltpu.VMEM((2, 2, 128, WIDTH), F32),
            pltpu.VMEM((2, 2, 128, WIDTH), F32),
            pltpu.VMEM((8, 2, 2, 128, WIDTH), F32),
            pltpu.VMEM((8, 2, 2, 128, WIDTH), F32),
            pltpu.VMEM((16, 384, 2 * WIDTH), BF16),
            pltpu.VMEM((2, TILE, WIDTH), F32),
            pltpu.VMEM((2, TILE, WIDTH), F32),
            pltpu.VMEM((TILE, WIDTH), F32),
            pltpu.VMEM((4, 128, WIDTH), F32),
            pltpu.VMEM((4, 128, WIDTH), F32),
            pltpu.VMEM((128, WIDTH), F32),
            pltpu.VMEM((CAP + 1, 32, WIDTH), F32),
            pltpu.SemaphoreType.DMA((NCOPY + 4,)),
            pltpu.SemaphoreType.DMA((NCOPY + 4,)),
            pltpu.SemaphoreType.DMA((3,)),
        ],
        compiler_params=pltpu.CompilerParams(
            collective_id=0, has_side_effects=True, vmem_limit_bytes=48 * 1024 * 1024
        ),
    )(index, blocks(h_values), blocks(p_values), blocks(s_values))
    return out.reshape(1, CAP, BS * BS)


def solution(mesh):
    tile = P("row", "col", None)
    flat = P("row", "col")
    in_specs = (tile, flat, flat) * 3 + (flat, flat)
    return jax.shard_map(shards, mesh=mesh, in_specs=in_specs, out_specs=tile, check_vma=False)
```

time: 405 us -> 116 us (0.29)
  the two profiles are of different devices: /device:TPU:61 before, /device:TPU:15 now
where the time goes in v1:
time: 116 us
  Pallas kernels  108 us (93%)
  local copies, waits for them, and re-layouts  4.83 us (4%)
  between operations  2.69 us (2%)
    pallas_call x1, Pallas kernels, shards(): pl.pallas_call(kernel, out_shape=jax.ShapeDtypeStruct((CAP, 32, WIDTH), F...  108 us
    unnamed x15, local copies, waits for them, and re-layouts  3.99 us

profile of v1, /device:TPU:15, one launch (start us, length us, event | category | flops | bytes accessed | tf_op | source)
XLA Modules:
  0.0 115.7 jit_solution(16411791219665732078)
XLA Ops:
  2.6 0.0 copy-start.4
  2.6 0.6 copy-done.4
  3.3 0.1 select_reduce_fusion.3
  3.4 0.0 copy-start.2
  3.4 0.0 copy-start.3
  3.4 0.6 copy-done.2
  4.0 0.0 copy-done.3
  4.0 0.1 select_reduce_fusion.1
  4.1 0.0 copy-start.5
  4.2 0.6 copy-done.5
  4.8 0.1 select_reduce_fusion
  4.9 0.1 concatenate.3.index_ref
  5.0 0.0 copy-start
  5.0 1.0 copy.12
  6.0 0.0 copy-done
  6.1 0.0 copy-start.1
  6.1 0.1 copy.13
  6.1 0.9 copy-done.1
  7.0 0.1 copy.14
  7.1 107.9 %shard_map.109 = f32[16,32,128]{2,1,0:T(8,128)S(1)} custom-call(s32[80]{0:T(128)S(1)} %concatenate.3.index_ref, f32[16,32,128]{2,1,0:T(8,128)S(1)} %bitcast.23, f32[16,32,128]{2,1,0:T(8,128)S(1)} %bitcast.24, f32[16,32,128]{2,1,0:T(8,128)S(1)} %bitcast.25), custom_call_target="tpu_custom_call" | custom-call | tf_op jit(solution)/shard_map/pallas_call | solution.py:392
  115.0 0.8 reshape.39
  (6 shorter events, 0.0 us)
Async XLA Ops:
  2.6 0.7 copy-start.4
  3.4 0.7 copy-start.2
  3.4 0.7 copy-start.3
  4.1 0.7 copy-start.5
  5.0 1.1 copy-start
  6.1 1.0 copy-start.1

commit v2 on v1

v2 whole, which is shorter than its diff:
```python
import jax
import jax.numpy as jnp
from jax import lax
from jax.experimental import pallas as pl
from jax.experimental.pallas import tpu as pltpu
from jax.sharding import PartitionSpec as P

MESH = pl.DeviceIdType.MESH
F32 = jnp.float32
BF16 = jnp.bfloat16
BS = 64
CAP = 16
TILE = 512
WIDTH = 128
HALF = 256
QUARTER = 128
NCOPY = 208


def split(value):
    high = value.astype(BF16)
    return high, (value - high.astype(F32)).astype(BF16)


def kernel(
    hp_ref, hc_ref, pp_ref, pc_ref, sp_ref, sc_ref, xp_ref, xc_ref, h_ref, p_ref, s_ref, out_ref,
    hp, hc, pp, pc, sp, sc, xp, xc, index_ref, raw, hv, pv, sv, hb, yb, pt, st, pb, sb, rhs_p, rhs_s, acc, part, xt, xs, tr, zt, bl,
    im, send_sem, recv_sem, local_sem, load_sem,
):
    loads = [
        pltpu.make_async_copy(src, dst, load_sem.at[n])
        for n, (src, dst) in enumerate((
            (hp_ref, hp), (hc_ref, hc), (pp_ref, pp), (pc_ref, pc), (sp_ref, sp), (sc_ref, sc),
            (xp_ref, xp), (xc_ref, xc), (h_ref, raw.at[0]), (p_ref, raw.at[1]), (s_ref, raw.at[2]),
        ))
    ]
    for load in loads:
        load.start()
    z = lax.axis_index("row")
    col = lax.axis_index("col")
    q = lax.rem(col, 2)
    y = lax.rem(col // 2, 4)
    x = col // 8
    lane = lax.broadcasted_iota(jnp.int32, (32, WIDTH), 1)
    low = lane < BS

    def device(dz, dx, dy):
        return (
            lax.rem(z + dz, 8),
            lax.rem(x + dx, 4) * 8 + lax.rem(y + dy, 4) * 2 + q,
        )

    partner = (z, col + 1 - 2 * q)
    mirror_row = col // 4

    own_place = lax.rem(col, 4)

    panel = mirror_row
    middle = (z, 4 * lax.rem(z + panel, 8) + own_place)
    giver = (z, 4 * lax.rem(panel - z + 8, 8) + own_place)

    def final(g):
        return (lax.rem(panel - z + 8, 8), 4 * z + g)

    def relay(k):
        return (panel, 4 * lax.rem(z + panel, 8) + k)

    def other(device_id):
        return jnp.logical_or(device_id[0] != z, device_id[1] != col)

    barrier = pltpu.get_barrier_semaphore()
    for target in (
        device(0, 0, 1), device(0, 0, 3), device(0, 1, 0), device(0, 3, 0),
        device(1, 0, 0), device(7, 0, 0), partner,
    ):
        pl.semaphore_signal(barrier, inc=1, device_id=target, device_id_type=MESH)
    for target in (giver, *(relay(k) for k in range(4))):
        @pl.when(other(target))
        def _(target=target):
            pl.semaphore_signal(barrier, inc=1, device_id=target, device_id_type=MESH)
    expected = 7 + jnp.where(other(middle), 1, 0)
    for g in range(4):
        expected = expected + jnp.where(other(final(g)), 1, 0)

    used = {}

    def copy(name, src, dst, target):
        if name not in used:
            used[name] = len(used)
        n = used[name]
        return pltpu.make_async_remote_copy(
            src_ref=src, dst_ref=dst, send_sem=send_sem.at[n], recv_sem=recv_sem.at[n],
            device_id=target, device_id_type=MESH,
        )

    started, gifts = [], []

    def send(name, src, dst, target, kept=None):
        made = copy(name, src, dst, target)
        made.start()
        (started if kept is None else kept).append(made)

    def arrived(name, dst):
        copy(name, dst, dst, partner).wait_recv()

    def place_rows(values, base, dst, index):
        @pl.loop(0, 8)
        def _(i):
            a = values[index_ref[base + 2 * i]]
            b = values[index_ref[base + 2 * i + 1]]
            top = jnp.where(low, a, pltpu.roll(b, BS, 1))
            bottom = jnp.where(low, pltpu.roll(a, BS, 1), b)
            start = pl.multiple_of(i * BS, BS)
            dst[index, pl.ds(start, 32), :] = top
            dst[index, pl.ds(start + 32, 32), :] = bottom

    def place_natural(values, base, dst):
        for i in range(8):
            a = values[index_ref[base + 2 * i]]
            b = values[index_ref[base + 2 * i + 1]]
            even = jnp.where(low, a, pltpu.roll(b, BS, 1))
            odd = jnp.where(low, pltpu.roll(a, BS, 1), b)
            g = i // 2
            view = dst.at[g % 2, g // 2]
            view[pl.ds((i % 2) * BS, 32, 2), :] = even
            view[pl.ds((i % 2) * BS + 1, 32, 2), :] = odd

    for load in loads:
        load.wait()
    for m, (places, counts) in enumerate(((hp, hc), (pp, pc), (sp, sc), (xp, xc))):
        count = counts[0, 0]

        @pl.loop(0, CAP)
        def _(place, m=m, places=places, count=count):
            slot = CAP
            for k in range(CAP):
                slot = jnp.where(jnp.logical_and(places[0, k] == place, k < count), k, slot)
            index_ref[m * CAP + place] = slot

    @pl.loop(0, CAP)
    def _(slot):
        index_ref[4 * CAP + slot] = jnp.where(slot < xc[0, 0], xp[0, slot], CAP)

    for m, values in enumerate((hv, pv, sv)):
        values[pl.ds(0, CAP)] = raw[m, 0].reshape(CAP, 32, WIDTH)
        values[CAP] = jnp.zeros((32, WIDTH), F32)
    here = x * 4 + y
    place_rows(hv, 0, hb, here)
    place_natural(pv, CAP, pt)
    place_natural(sv, 2 * CAP, st)

    pl.semaphore_wait(barrier, expected)

    def tile_at(first, a, b):
        dy, dx = (a, b) if first == 1 else (b, a)
        return lax.rem(x + dx, 4) * 4 + lax.rem(y + dy, 4)

    def step(first, stage, by):
        along_y = (first == 1) == (stage == 1)
        return device(0, 0, by) if along_y else device(0, by, 0)

    def whole(buf, part, side, a, b):
        return buf.at[tile_at(1 - side, a, b), pl.ds(part * HALF + side * QUARTER, QUARTER)]

    def piece(buf, part, side, a, b, k):
        start = part * HALF + side * QUARTER + k * BS
        return buf.at[tile_at(1 - side, a, b), pl.ds(start, BS)]

    def second_out(tag, buf, part, side, a):
        src = whole(buf, part, side, a, 0)
        for by in (1, 3):
            send((tag, part, side, "s2", a, by), src, src, step(1 - side, 2, by))

    def out(tag, buf, part):
        for side in range(2):
            src = whole(buf, part, side, 0, 0)
            for by in (1, 3):
                send((tag, part, side, "s1", by), src, src, step(1 - side, 1, by))
        for side in range(2):
            second_out(tag, buf, part, side, 0)

    def first_in(tag, buf, part):
        for by, a, k in ((1, 3, 0), (3, 1, 1)):
            for side in range(2):
                arrived((tag, part, side, "s1", by), whole(buf, part, side, a, 0))
                src = piece(buf, part, side, a, 0, k)
                send((tag, part, side, "f1", by), src, src, step(1 - side, 1, by))
                second_out(tag, buf, part, side, a)

    def first_far(tag, buf, part):
        for side in range(2):
            for by, k in ((1, 0), (3, 1)):
                arrived((tag, part, side, "f1", by), piece(buf, part, side, 2, 0, k))
            second_out(tag, buf, part, side, 2)

    def second_in(tag, buf, part, a):
        for by, b, k in ((1, 3, 0), (3, 1, 1)):
            for side in range(2):
                arrived((tag, part, side, "s2", a, by), whole(buf, part, side, a, b))
                src = piece(buf, part, side, a, b, k)
                send((tag, part, side, "f2", a, by), src, src, step(1 - side, 2, by))

    def second_far(tag, buf, part):
        for a in (0, 3, 1, 2):
            for side in range(2):
                for by, k in ((1, 0), (3, 1)):
                    arrived((tag, part, side, "f2", a, by), piece(buf, part, side, a, 2, k))

    def ring_start(tag, own, buf):
        keep = pltpu.make_async_copy(own.at[q], buf.at[z, q], local_sem.at[0 if tag == "p" else 1])
        keep.start()
        send((tag, "mate"), own.at[1 - q], buf.at[z, q], partner)
        for by in (1, 7):
            send((tag, "own", by, 1), own.at[q], buf.at[z, q], device(by, 0, 0))
        return keep

    def ring_mate(tag, buf):
        arrived((tag, "mate"), buf.at[z, 1 - q])
        src = buf.at[z, 1 - q]
        for by in (1, 7):
            send((tag, "other", by, 1), src, src, device(by, 0, 0))

    def ring_in(tag, buf, d):
        for kind, core in (("own", q), ("other", 1 - q)):
            for by in (1, 7):
                away = lax.rem(z + (8 - by) * d, 8)
                if d < 4:
                    arrived((tag, kind, by, d), buf.at[away, core])
                if d < 3:
                    src = buf.at[away, core]
                    send((tag, kind, by, d + 1), src, src, device(by, 0, 0))
                elif d == 3:
                    src = buf.at[away, core, 0 if by == 1 else 1]
                    send((tag, kind, by, 4), src, src, device(by, 0, 0))
                else:
                    arrived((tag, kind, by, 4), buf.at[away, core, 0 if by == 1 else 1])

    def weights(buf, rhs, away):
        for g in range(2):
            wide = jnp.concatenate([buf[away, 0, g], buf[away, 1, g]], axis=1)
            high, rest = split(wide)
            t = 2 * away + g
            rhs[t, pl.ds(0, 128), :] = high
            rhs[t, pl.ds(128, 128), :] = high
            rhs[t, pl.ds(256, 128), :] = rest

    def weights_at(buf, rhs, d):
        @pl.loop(0, 2 if d < 4 else 1)
        def _(k):
            weights(buf, rhs, lax.rem(z + jnp.where(k == 0, d, 8 - d), 8))

    def product(buf, rhs, half):
        rows = pl.ds(half * HALF, HALF)
        acc[0, rows, :] = jnp.zeros((HALF, WIDTH), F32)
        acc[1, rows, :] = jnp.zeros((HALF, WIDTH), F32)

        @pl.loop(0, 2)
        def _(t):
            parts = []
            for k in range(8):
                high, rest = split(buf[8 * t + k, rows, :])
                parts += [high, rest, high]
            term = jnp.dot(
                jnp.concatenate(parts, axis=1),
                rhs[pl.ds(8 * t, 8)].reshape(8 * 384, 2 * WIDTH),
                preferred_element_type=F32,
            )
            acc[0, rows, :] += term[:, :WIDTH]
            acc[1, rows, :] += term[:, WIDTH:]

    def give(tag, half):
        rows = pl.ds(half * HALF, HALF)
        send((tag, half), acc.at[1 - q, rows], part.at[0 if tag == "dy" else 1, rows], partner,
             gifts if tag == "dy" else None)

    def masked(half):
        rows = pl.ds(half * HALF, HALF)
        arrived(("dy", half), part.at[0, rows])
        wide = lax.broadcasted_iota(jnp.int32, (BS, WIDTH), 1)
        for i in range(4 * half, 4 * half + 4):
            kept = jnp.where(wide < BS, index_ref[3 * CAP + 2 * i], index_ref[3 * CAP + 2 * i + 1]) < CAP
            strip = pl.ds(i * BS, BS)
            yb[here, strip, :] = jnp.where(kept, acc[q, strip, :] + part[0, strip, :], 0.0)
        out("y", yb, half)

    out("h", hb, 0)
    keep_p = ring_start("p", pt, pb)
    ring_mate("p", pb)
    first_in("h", hb, 0)
    out("h", hb, 1)
    keep_p.wait()
    weights(pb, rhs_p, z)
    second_in("h", hb, 0, 0)
    ring_in("p", pb, 1)
    first_far("h", hb, 0)
    first_in("h", hb, 1)
    weights_at(pb, rhs_p, 1)
    second_in("h", hb, 0, 3)
    second_in("h", hb, 0, 1)
    second_in("h", hb, 1, 0)
    ring_in("p", pb, 2)
    first_far("h", hb, 1)
    weights_at(pb, rhs_p, 2)
    second_in("h", hb, 0, 2)
    second_far("h", hb, 0)
    second_in("h", hb, 1, 3)
    second_in("h", hb, 1, 1)
    ring_in("p", pb, 3)
    keep_s = ring_start("s", st, sb)
    ring_mate("s", sb)
    weights_at(pb, rhs_p, 3)
    second_in("h", hb, 1, 2)
    ring_in("p", pb, 4)
    weights_at(pb, rhs_p, 4)
    product(hb, rhs_p, 0)
    give("dy", 0)
    second_far("h", hb, 1)
    product(hb, rhs_p, 1)
    give("dy", 1)

    masked(0)
    keep_s.wait()
    weights(sb, rhs_s, z)
    first_in("y", yb, 0)
    masked(1)
    ring_in("s", sb, 1)
    weights_at(sb, rhs_s, 1)
    second_in("y", yb, 0, 0)
    first_far("y", yb, 0)
    first_in("y", yb, 1)
    ring_in("s", sb, 2)
    weights_at(sb, rhs_s, 2)
    second_in("y", yb, 0, 3)
    second_in("y", yb, 0, 1)
    second_in("y", yb, 1, 0)
    first_far("y", yb, 1)
    ring_in("s", sb, 3)
    weights_at(sb, rhs_s, 3)
    second_in("y", yb, 0, 2)
    second_in("y", yb, 1, 3)
    second_in("y", yb, 1, 1)
    second_far("y", yb, 0)
    ring_in("s", sb, 4)
    weights_at(sb, rhs_s, 4)
    gifts[0].wait_send()
    product(yb, rhs_s, 0)
    give("dx", 0)
    second_in("y", yb, 1, 2)
    gifts[1].wait_send()

    def to_middle(g):
        return pltpu.make_async_remote_copy(
            src_ref=xs.at[g], dst_ref=im.at[g], send_sem=send_sem.at[NCOPY + g],
            recv_sem=recv_sem.at[NCOPY + g], device_id=middle, device_id_type=MESH,
        )

    def onward(g):
        return pltpu.make_async_remote_copy(
            src_ref=im.at[g], dst_ref=tr.at[own_place], send_sem=send_sem.at[NCOPY + 4 + g],
            recv_sem=recv_sem.at[NCOPY + 4 + own_place], device_id=final(g), device_id_type=MESH,
        )

    def stay(src, dst):
        copied = pltpu.make_async_copy(src, dst, local_sem.at[2])
        copied.start()
        copied.wait()

    def either(away, there, here_):
        pl.when(away)(there)
        pl.when(jnp.logical_not(away))(here_)

    def chunks_out(half):
        arrived(("dx", half), part.at[1, pl.ds(half * HALF, HALF)])
        for g in (2 * half, 2 * half + 1):
            for k in range(2):
                base = g * QUARTER + k * BS
                for odd in range(2):
                    strip = pl.ds(base + 32 * odd, 32)
                    value = acc[q, strip, :] + part[1, strip, :]
                    xt[strip, :] = value
                    xs[g, pl.ds(k * BS + odd, 32, 2), :] = value
            either(
                other(middle),
                lambda g=g: to_middle(g).start(),
                lambda g=g: stay(xs.at[g], im.at[g]),
            )

    def chunks_on(half):
        for g in (2 * half, 2 * half + 1):
            @pl.when(other(giver))
            def _(g=g):
                to_middle(g).wait_recv()

            either(
                other(final(g)),
                lambda g=g: onward(g).start(),
                lambda g=g: stay(im.at[g], tr.at[g]),
            )

    chunks_out(0)
    second_far("y", yb, 1)
    product(yb, rhs_s, 1)
    give("dx", 1)
    chunks_on(0)
    chunks_out(1)
    chunks_on(1)

    bl[CAP] = jnp.zeros((32, WIDTH), F32)
    for g in range(4):
        @pl.when(other(relay(g)))
        def _(g=g):
            pltpu.make_async_remote_copy(
                src_ref=tr.at[g], dst_ref=tr.at[g], send_sem=send_sem.at[NCOPY + 4 + g],
                recv_sem=recv_sem.at[NCOPY + 4 + g], device_id=partner, device_id_type=MESH,
            ).wait_recv()

        zt[...] = tr[g].T
        for k in range(2):
            i = 2 * g + k
            top = xt[pl.ds(i * BS, 32), :] + zt[pl.ds(k * BS, 32, 2), :]
            bottom = xt[pl.ds(i * BS + 32, 32), :] + zt[pl.ds(k * BS + 1, 32, 2), :]
            bl[2 * i] = jnp.where(low, top, pltpu.roll(bottom, BS, 1))
            bl[2 * i + 1] = jnp.where(low, pltpu.roll(top, BS, 1), bottom)

    @pl.loop(0, CAP)
    def _(slot):
        out_ref[slot] = bl[index_ref[4 * CAP + slot]]

    for g in range(4):
        @pl.when(other(middle))
        def _(g=g):
            to_middle(g).wait_send()

        @pl.when(other(final(g)))
        def _(g=g):
            onward(g).wait_send()

    for made in started:
        made.wait_send()


def shards(
    h_values, h_places, h_counts, p_values, p_places, p_counts,
    s_values, s_places, s_counts, x_places, x_counts,
):
    vmem = pl.BlockSpec(memory_space=pltpu.VMEM)
    anywhere = pl.BlockSpec(memory_space=pl.ANY)
    out = pl.pallas_call(
        kernel,
        out_shape=jax.ShapeDtypeStruct((CAP, 32, WIDTH), F32),
        in_specs=[anywhere] * 11,
        out_specs=vmem,
        scratch_shapes=[
            pltpu.SMEM((1, CAP), jnp.int32), pltpu.SMEM((1, 1), jnp.int32),
            pltpu.SMEM((1, CAP), jnp.int32), pltpu.SMEM((1, 1), jnp.int32),
            pltpu.SMEM((1, CAP), jnp.int32), pltpu.SMEM((1, 1), jnp.int32),
            pltpu.SMEM((1, CAP), jnp.int32), pltpu.SMEM((1, 1), jnp.int32),
            pltpu.SMEM((5 * CAP,), jnp.int32),
            pltpu.VMEM((3, 1, CAP, BS * BS), F32),
            pltpu.VMEM((CAP + 1, 32, WIDTH), F32),
            pltpu.VMEM((CAP + 1, 32, WIDTH), F32),
            pltpu.VMEM((CAP + 1, 32, WIDTH), F32),
            pltpu.VMEM((16, TILE, WIDTH), F32),
            pltpu.VMEM((16, TILE, WIDTH), F32),
            pltpu.VMEM((2, 2, 128, WIDTH), F32),
            pltpu.VMEM((2, 2, 128, WIDTH), F32),
            pltpu.VMEM((8, 2, 2, 128, WIDTH), F32),
            pltpu.VMEM((8, 2, 2, 128, WIDTH), F32),
            pltpu.VMEM((16, 384, 2 * WIDTH), BF16),
            pltpu.VMEM((16, 384, 2 * WIDTH), BF16),
            pltpu.VMEM((2, TILE, WIDTH), F32),
            pltpu.VMEM((2, TILE, WIDTH), F32),
            pltpu.VMEM((TILE, WIDTH), F32),
            pltpu.VMEM((4, 128, WIDTH), F32),
            pltpu.VMEM((4, 128, WIDTH), F32),
            pltpu.VMEM((128, WIDTH), F32),
            pltpu.VMEM((CAP + 1, 32, WIDTH), F32),
            pltpu.VMEM((4, 128, WIDTH), F32),
            pltpu.SemaphoreType.DMA((NCOPY + 8,)),
            pltpu.SemaphoreType.DMA((NCOPY + 8,)),
            pltpu.SemaphoreType.DMA((3,)),
            pltpu.SemaphoreType.DMA((11,)),
        ],
        compiler_params=pltpu.CompilerParams(
            collective_id=0, has_side_effects=True, vmem_limit_bytes=48 * 1024 * 1024
        ),
    )(
        h_places, h_counts, p_places, p_counts, s_places, s_counts, x_places, x_counts,
        h_values, p_values, s_values,
    )
    return out.reshape(1, CAP, BS * BS)


def solution(mesh):
    tile = P("row", "col", None)
    flat = P("row", "col")
    in_specs = (tile, flat, flat) * 3 + (flat, flat)
    return jax.shard_map(shards, mesh=mesh, in_specs=in_specs, out_specs=tile, check_vma=False)
```

time: 116 us -> 100 us (0.86)
  the two profiles are of different devices: /device:TPU:15 before, /device:TPU:61 now
where the time goes in v2:
time: 100 us; the launch traced here: 99.8 us
  Pallas kernels  93.5 us (94%)
  local copies, waits for them, and re-layouts  3.61 us (4%)
  between operations  2.71 us (3%)
    pallas_call x1, Pallas kernels, shards(): pl.pallas_call(kernel, out_shape=jax.ShapeDtypeStruct((CAP, 32, WIDTH), F...  93.5 us
    unnamed x14, local copies, waits for them, and re-layouts  2.86 us

profile of v2, /device:TPU:61, one launch (start us, length us, event | category | flops | bytes accessed | tf_op | source)
XLA Modules:
  0.0 99.8 jit_solution(15714391962179734620)
XLA Ops:
  1.3 0.0 copy-start.6
  2.0 0.0 copy-start.3
  2.0 0.0 copy-start.4
  2.0 0.0 copy-start.5
  2.7 0.0 copy-done.6
  2.7 0.0 copy-done.3
  2.7 0.0 copy-done.4
  2.7 0.0 copy-done.5
  2.7 0.0 copy-start
  2.7 0.9 copy-done
  3.7 0.0 copy-start.1
  3.7 0.9 copy-done.1
  4.6 0.0 copy-start.2
  4.6 0.9 copy-done.2
  5.6 93.5 %shard_map.109 = f32[16,32,128]{2,1,0:T(8,128)S(1)} custom-call(s32[1,16]{1,0:T(1,128)S(1)} %copy-done.3, s32[1,1]{1,0:T(1,128)S(6)} %copy.12.hc_ref, s32[1,16]{1,0:T(1,128)S(1)} %copy-done.4, s32[1,1]{1,0:T(1,128)S(6)} %copy.13.pc_ref, s32[1,16]{1,0:T(1,128)S(1)} %copy-done.5, s32[1,1]{1,0:T(1,128)S(6)} %copy.14.sc_ref, s32[1,16]{1,0:T(1,128)S(1)} %copy-done.6, ...), custom_call_target="tpu_custom_call" | custom-call | tf_op jit(solution)/shard_map/pallas_call | solution.py:448
  99.0 0.8 reshape.3
Async XLA Ops:
  1.3 1.4 %copy-start.6 = (s32[1,16]{1,0:T(1,128)S(1)}, s32[1,16]{1,0:T(1,128)}, u32[]{:S(2)}) copy-start(s32[1,16]{1,0:T(1,128)} %xp_ref.1) | copy-start | bytes 196
  2.0 0.7 copy-start.3
  2.0 0.7 copy-start.4
  2.0 0.7 copy-start.5
  2.7 1.0 copy-start
  3.7 0.9 copy-start.1
  4.6 0.9 copy-start.2

commit v3 on v2

--- a/solution.py
+++ b/solution.py
@@ -14,7 +14,8 @@
 WIDTH = 128
 HALF = 256
 QUARTER = 128
-NCOPY = 208
+NCOPY = 198
+POOL = 48
 
 
 def split(value):
@@ -82,23 +83,26 @@
     for g in range(4):
         expected = expected + jnp.where(other(final(g)), 1, 0)
 
-    used = {}
-
-    def copy(name, src, dst, target):
+    used, started, gifts = {}, [], []
+
+    def copy(name, src, dst, target, sent=0):
         if name not in used:
             used[name] = len(used)
-        n = used[name]
         return pltpu.make_async_remote_copy(
-            src_ref=src, dst_ref=dst, send_sem=send_sem.at[n], recv_sem=recv_sem.at[n],
+            src_ref=src, dst_ref=dst, send_sem=send_sem.at[sent], recv_sem=recv_sem.at[used[name]],
             device_id=target, device_id_type=MESH,
         )
 
-    started, gifts = [], []
-
     def send(name, src, dst, target, kept=None):
-        made = copy(name, src, dst, target)
+        if kept is None:
+            if len(started) >= POOL:
+                started[-POOL].wait_send()
+            made = copy(name, src, dst, target, len(started) % POOL)
+            started.append(made)
+        else:
+            made = copy(name, src, dst, target, POOL + len(kept))
+            kept.append(made)
         made.start()
-        (started if kept is None else kept).append(made)
 
     def arrived(name, dst):
         copy(name, dst, dst, partner).wait_recv()
@@ -350,13 +354,13 @@
 
     def to_middle(g):
         return pltpu.make_async_remote_copy(
-            src_ref=xs.at[g], dst_ref=im.at[g], send_sem=send_sem.at[NCOPY + g],
+            src_ref=xs.at[g], dst_ref=im.at[g], send_sem=send_sem.at[POOL + 2 + g],
             recv_sem=recv_sem.at[NCOPY + g], device_id=middle, device_id_type=MESH,
         )
 
     def onward(g):
         return pltpu.make_async_remote_copy(
-            src_ref=im.at[g], dst_ref=tr.at[own_place], send_sem=send_sem.at[NCOPY + 4 + g],
+            src_ref=im.at[g], dst_ref=tr.at[own_place], send_sem=send_sem.at[POOL + 2 + 4 + g],
             recv_sem=recv_sem.at[NCOPY + 4 + own_place], device_id=final(g), device_id_type=MESH,
         )
 
@@ -410,7 +414,7 @@
         @pl.when(other(relay(g)))
         def _(g=g):
             pltpu.make_async_remote_copy(
-                src_ref=tr.at[g], dst_ref=tr.at[g], send_sem=send_sem.at[NCOPY + 4 + g],
+                src_ref=tr.at[g], dst_ref=tr.at[g], send_sem=send_sem.at[POOL + 2 + 4 + g],
                 recv_sem=recv_sem.at[NCOPY + 4 + g], device_id=partner, device_id_type=MESH,
             ).wait_recv()
 
@@ -435,7 +439,8 @@
         def _(g=g):
             onward(g).wait_send()
 
-    for made in started:
+    assert len(used) == NCOPY, len(used)
+    for made in started[-POOL:]:
         made.wait_send()
 
 
@@ -476,7 +481,7 @@
             pltpu.VMEM((128, WIDTH), F32),
             pltpu.VMEM((CAP + 1, 32, WIDTH), F32),
             pltpu.VMEM((4, 128, WIDTH), F32),
-            pltpu.SemaphoreType.DMA((NCOPY + 8,)),
+            pltpu.SemaphoreType.DMA((POOL + 10,)),
             pltpu.SemaphoreType.DMA((NCOPY + 8,)),
             pltpu.SemaphoreType.DMA((3,)),
             pltpu.SemaphoreType.DMA((11,)),

time: 100 us -> 98.3 us (0.983)
  Pallas kernels: 93.5 us -> 91.8 us
    pallas_call x1, Pallas kernels: 93.5 us -> 91.8 us  [shards(): pl.pallas_call(kernel, out_shape=jax.ShapeDtypeStruct((CAP, 32, WIDTH), F...]
where the time goes in v3:
time: 98.3 us; the launch traced here: 98.1 us
  Pallas kernels  91.8 us (93%)
  local copies, waits for them, and re-layouts  3.61 us (4%)
  between operations  2.71 us (3%)
    pallas_call x1, Pallas kernels, shards(): pl.pallas_call(kernel, out_shape=jax.ShapeDtypeStruct((CAP, 32, WIDTH), F...  91.8 us
    unnamed x14, local copies, waits for them, and re-layouts  2.86 us

profile of v3, /device:TPU:61, one launch (start us, length us, event | category | flops | bytes accessed | tf_op | source)
XLA Modules:
  0.0 98.1 jit_solution(1558922610771950178)
XLA Ops:
  1.3 0.0 copy-start.6
  2.0 0.0 copy-start.3
  2.0 0.0 copy-start.4
  2.0 0.0 copy-start.5
  2.7 0.0 copy-done.6
  2.7 0.0 copy-done.3
  2.7 0.0 copy-done.4
  2.7 0.0 copy-done.5
  2.7 0.0 copy-start
  2.7 0.9 copy-done
  3.7 0.0 copy-start.1
  3.7 0.9 copy-done.1
  4.6 0.0 copy-start.2
  4.6 0.9 copy-done.2
  5.6 91.8 %shard_map.109 = f32[16,32,128]{2,1,0:T(8,128)S(1)} custom-call(s32[1,16]{1,0:T(1,128)S(1)} %copy-done.3, s32[1,1]{1,0:T(1,128)S(6)} %copy.12.hc_ref, s32[1,16]{1,0:T(1,128)S(1)} %copy-done.4, s32[1,1]{1,0:T(1,128)S(6)} %copy.13.pc_ref, s32[1,16]{1,0:T(1,128)S(1)} %copy-done.5, s32[1,1]{1,0:T(1,128)S(6)} %copy.14.sc_ref, s32[1,16]{1,0:T(1,128)S(1)} %copy-done.6, ...), custom_call_target="tpu_custom_call" | custom-call | tf_op jit(solution)/shard_map/pallas_call | solution.py:453
  97.4 0.8 reshape.3
Async XLA Ops:
  1.3 1.4 %copy-start.6 = (s32[1,16]{1,0:T(1,128)S(1)}, s32[1,16]{1,0:T(1,128)}, u32[]{:S(2)}) copy-start(s32[1,16]{1,0:T(1,128)} %xp_ref.1) | copy-start | bytes 196
  2.0 0.7 copy-start.3
  2.0 0.7 copy-start.4
  2.0 0.7 copy-start.5
  2.7 1.0 copy-start
  3.7 0.9 copy-start.1
  4.6 0.9 copy-start.2

commit v4 on v3

--- a/solution.py
+++ b/solution.py
@@ -75,14 +75,6 @@
         device(1, 0, 0), device(7, 0, 0), partner,
     ):
         pl.semaphore_signal(barrier, inc=1, device_id=target, device_id_type=MESH)
-    for target in (giver, *(relay(k) for k in range(4))):
-        @pl.when(other(target))
-        def _(target=target):
-            pl.semaphore_signal(barrier, inc=1, device_id=target, device_id_type=MESH)
-    expected = 7 + jnp.where(other(middle), 1, 0)
-    for g in range(4):
-        expected = expected + jnp.where(other(final(g)), 1, 0)
-
     used, started, gifts = {}, [], []
 
     def copy(name, src, dst, target, sent=0):
@@ -153,7 +145,7 @@
     place_natural(pv, CAP, pt)
     place_natural(sv, 2 * CAP, st)
 
-    pl.semaphore_wait(barrier, expected)
+    pl.semaphore_wait(barrier, 7)
 
     def tile_at(first, a, b):
         dy, dx = (a, b) if first == 1 else (b, a)

time: 98.3 us -> 98.8 us (level)
  no operation moved by 1% of the time
where the time goes in v4:
time: 98.8 us; the launch traced here: 98.6 us
  Pallas kernels  92.3 us (93%)
  local copies, waits for them, and re-layouts  3.61 us (4%)
  between operations  2.71 us (3%)
    pallas_call x1, Pallas kernels, shards(): pl.pallas_call(kernel, out_shape=jax.ShapeDtypeStruct((CAP, 32, WIDTH), F...  92.3 us
    unnamed x14, local copies, waits for them, and re-layouts  2.86 us

profile of v4, /device:TPU:61, one launch (start us, length us, event | category | flops | bytes accessed | tf_op | source)
XLA Modules:
  0.0 98.6 jit_solution(12398215115108121924)
XLA Ops:
  1.3 0.0 copy-start.6
  2.0 0.0 copy-start.3
  2.0 0.0 copy-start.4
  2.0 0.0 copy-start.5
  2.7 0.0 copy-done.6
  2.7 0.0 copy-done.3
  2.7 0.0 copy-done.4
  2.7 0.0 copy-done.5
  2.7 0.0 copy-start
  2.7 0.9 copy-done
  3.7 0.0 copy-start.1
  3.7 0.9 copy-done.1
  4.6 0.0 copy-start.2
  4.6 0.9 copy-done.2
  5.6 92.3 %shard_map.109 = f32[16,32,128]{2,1,0:T(8,128)S(1)} custom-call(s32[1,16]{1,0:T(1,128)S(1)} %copy-done.3, s32[1,1]{1,0:T(1,128)S(6)} %copy.12.hc_ref, s32[1,16]{1,0:T(1,128)S(1)} %copy-done.4, s32[1,1]{1,0:T(1,128)S(6)} %copy.13.pc_ref, s32[1,16]{1,0:T(1,128)S(1)} %copy-done.5, s32[1,1]{1,0:T(1,128)S(6)} %copy.14.sc_ref, s32[1,16]{1,0:T(1,128)S(1)} %copy-done.6, ...), custom_call_target="tpu_custom_call" | custom-call | tf_op jit(solution)/shard_map/pallas_call | solution.py:445
  97.9 0.8 reshape.3
Async XLA Ops:
  1.3 1.4 %copy-start.6 = (s32[1,16]{1,0:T(1,128)S(1)}, s32[1,16]{1,0:T(1,128)}, u32[]{:S(2)}) copy-start(s32[1,16]{1,0:T(1,128)} %xp_ref.1) | copy-start | bytes 196
  2.0 0.7 copy-start.3
  2.0 0.7 copy-start.4
  2.0 0.7 copy-start.5
  2.7 1.0 copy-start
  3.7 0.9 copy-start.1
  4.6 0.9 copy-start.2
